TPU v7x, 1024 devices: a whole 4x4x32 slice. The times are simulated.
1024 devices in a mesh: tm: 128 (over z, x_lo, core), op: 8 (over x_hi, y).
Axes of the slice: x: 4 (x_hi: 2, x_lo: 2; x = x_hi * 2 + x_lo), y: 4, z: 32, core: 2. Of those that a mesh axis runs over, the one named last changes fastest.
Arguments:
- sink_fields: bfloat16 [128, 2, 2, 512, 512], P('tm', None, None, 'op'), may hold values from -0.1875 to 0.1875
- source_fields: bfloat16 [128, 2, 2, 512, 512], P('tm', None, None, 'op'), may hold values from -0.1875 to 0.1875
- source_live: int32 [128], P('tm'), may hold values 0 or 1
- chain_factors: int32 [128, 4], replicated, may hold values from 0 to 1
- chain_target: int32 [128], replicated, may hold values from 0 to 15
Outputs:
- correlators: float32 [2, 16, 2], replicated
All inputs are finite; a program needn't handle non-finite values. No bound on the sum of `source_live` on one device may be relied on, other than what follows from the above.
Results may differ from a plain program's by a relative error of at most 0.0039.
Values may be sent and summed in bfloat16 or wider, within the bound.
A program may use at most 32 MiB of HBM per device.

v0:
```python
import functools
import math

import jax
import jax.numpy as jnp
from jax import lax
from jax.sharding import Mesh
from jax.sharding import PartitionSpec as P

WIN = 2
NCORR = 16
OP = ("op_0", "op_1")
TM = ("tm_0", "tm_1", "tm_2")
TM_OP = ("tm_0", "tm_1", "tm_2", "op_0", "op_1")


def in_order(pieces, dim):
    shape = list(pieces.shape[1:])
    shape[dim] *= pieces.shape[0]
    return jnp.moveaxis(pieces, 0, dim).reshape(shape)


def sent_to_all(array, axis):
    copies = jnp.broadcast_to(array, (lax.axis_size(axis), *array.shape))
    return lax.all_to_all(copies, axis, split_axis=0, concat_axis=0, tiled=True)


def collect(array, axis, dim):
    return in_order(sent_to_all(array, axis), dim)


def shifted(array, axis, by):
    devices = lax.axis_size(axis)
    return lax.ppermute(array, axis, [(i, (i + by) % devices) for i in range(devices)])


def by_axis(array, axes):
    return functools.reduce(lax.psum, axes, array)


def stacked_block(real_part, imag_part):
    upper_half = jnp.concatenate([real_part, imag_part], -1)
    lower_half = jnp.concatenate([-imag_part, real_part], -1)
    return jnp.concatenate([upper_half, lower_half], -2)


def pair_traces(sink_stack, sink_transposed, source_full, row_start, row_count, full_width):
    source_block = stacked_block(source_full[:, 0], source_full[:, 1])
    products = jnp.einsum(
        "arx,bxy->abry", sink_stack, source_block, preferred_element_type=jnp.float32
    ).astype(jnp.bfloat16)
    columns = lax.dynamic_slice_in_dim(source_full, row_start, row_count, 3)
    columns = jnp.swapaxes(columns, -1, -2)
    column_stack = jnp.concatenate([columns[:, 0], columns[:, 1]], -1)
    flipped = jnp.einsum(
        "dry,cyz->cdrz", column_stack, sink_transposed, preferred_element_type=jnp.float32
    ).astype(jnp.bfloat16)
    pair_count = products.shape[0] * products.shape[1]
    products = products.reshape(pair_count, row_count, 2 * full_width)
    flipped = flipped.reshape(pair_count, row_count, 2 * full_width)
    real_left = products[..., :full_width]
    imag_left = products[..., full_width:]
    real_right = flipped[..., :full_width]
    imag_right = flipped[..., full_width:]
    real_trace = jnp.einsum(
        "pij,qij->pq", real_left, real_right, preferred_element_type=jnp.float32
    ) - jnp.einsum("pij,qij->pq", imag_left, imag_right, preferred_element_type=jnp.float32)
    imag_trace = jnp.einsum(
        "pij,qij->pq", real_left, imag_right, preferred_element_type=jnp.float32
    ) + jnp.einsum("pij,qij->pq", imag_left, real_right, preferred_element_type=jnp.float32)
    return jnp.stack([real_trace.reshape(-1), imag_trace.reshape(-1)])


def per_device(sink_fields, source_fields, source_live, chain_factors, chain_target):
    field_count = sink_fields.shape[1]
    row_count = sink_fields.shape[3]
    full_width = sink_fields.shape[4]
    pair_count = field_count * field_count
    row_start = lax.axis_index(OP) * row_count
    sink_whole = collect(sink_fields, OP, 3)[0]
    sink_local = sink_fields[0]
    sink_stack = jnp.concatenate([sink_local[:, 0], sink_local[:, 1]], -1)
    sink_flipped = jnp.swapaxes(sink_whole, -1, -2)
    sink_transposed = stacked_block(sink_flipped[:, 0], sink_flipped[:, 1])
    chain_codes = (
        (chain_factors[:, 0] * field_count + chain_factors[:, 1]) * pair_count
        + chain_factors[:, 2] * field_count
        + chain_factors[:, 3]
    )
    chain_onehot = (
        chain_codes[:, None] == jnp.arange(pair_count * pair_count, dtype=jnp.int32)[None, :]
    ).astype(jnp.float32)
    target_onehot = (chain_target[:, None] == jnp.arange(NCORR, dtype=jnp.int32)[None, :]).astype(
        jnp.float32
    )
    selector = jnp.dot(target_onehot.T, chain_onehot, precision=lax.Precision.HIGHEST)
    live_now = source_live.astype(jnp.bfloat16)
    results = []
    block_now = source_fields
    for separation in range(WIN):
        block_now, live_now = shifted((block_now, live_now), TM, 1)
        source_now = collect(block_now, OP, 3)
        traces = pair_traces(
            sink_stack, sink_transposed, source_now[0], row_start, row_count, full_width
        )
        weight = live_now[0].astype(jnp.float32)
        results.append(weight * jnp.dot(traces, selector.T, precision=lax.Precision.HIGHEST))
    partial_sums = jnp.stack(results, -1)
    totals = by_axis(partial_sums, TM_OP)
    return totals / math.sqrt(lax.axis_size(TM))


def solution(mesh):
    split = Mesh(mesh.devices.reshape(32, 2, 2, 2, 4), ("tm_0", "tm_1", "tm_2", "op_0", "op_1"))
    return jax.shard_map(
        per_device,
        mesh=split,
        in_specs=(P(TM, None, None, OP, None), P(TM, None, None, OP, None), P(TM), P(), P()),
        out_specs=P(),
        check_vma=False,
    )
```

profile of v0, /device:TPU:1, one launch (start us, length us, event | category | flops | bytes accessed | tf_op | source)
XLA Modules:
  0.0 217.2 jit_solution(10655831457560645921)
XLA Ops:
  0.0 2.5 %broadcast_in_dim.14 = bf16[8,1,2,2,64,512]{5,4,3,2,1,0:T(8,128)(2,1)} broadcast(bf16[2,2,64,512]{3,2,1,0:T(8,128)(2,1)} %bitcast.145), dimensions={2,3,4,5} | broadcast | bytes 2359296 | tf_op jit(solution)/shard_map/broadcast_in_dim | solution.py:24
  2.5 7.6 %all-to-all-start.1 = ((bf16[8,1,2,2,64,512]{5,4,3,2,1,0:T(8,128)(2,1)}), bf16[8,1,2,2,64,512]{5,4,3,2,1,0:T(8,128)(2,1)S(1)}, u32[]{:S(2)}, u32[]{:S(2)}) async-start(bf16[8,1,2,2,64,512]{5,4,3,2,1,0:T(8,128)(2,1)} %broadcast_in_dim.14), calls=%async_computation.1 | async-start | bytes 4194304 | tf_op jit(solution)/shard_map/all_to_all | solution.py:25
  10.1 3.1 %collective-permute-start.1 = (bf16[1,2,2,64,512]{4,3,2,1,0:T(8,128)(2,1)S(1)}, bf16[1,2,2,64,512]{4,3,2,1,0:T(8,128)(2,1)S(1)}, u32[]{:S(2)}, u32[]{:S(2)}) collective-permute-start(bf16[1,2,2,64,512]{4,3,2,1,0:T(8,128)(2,1)S(1)} %copy-done.7), channel_id=1, source_target_pairs={{0,8},{8,16},{16,24},{24,32},{32,40},{40,48},{48,56},{56,64},{64,7... | collective-permute-start | bytes 786440 | tf_op jit(solution)/shard_map/ppermute | solution.py:34
  13.2 15.4 %collective-permute-done.1 = bf16[1,2,2,64,512]{4,3,2,1,0:T(8,128)(2,1)S(1)} collective-permute-done((bf16[1,2,2,64,512]{4,3,2,1,0:T(8,128)(2,1)S(1)}, bf16[1,2,2,64,512]{4,3,2,1,0:T(8,128)(2,1)S(1)}, u32[]{:S(2)}, u32[]{:S(2)}) %collective-permute-start.1) | collective-permute-done | bytes 262176 | tf_op jit(solution)/shard_map/ppermute | solution.py:34
  28.6 1.6 broadcast_in_dim.6
  30.2 6.8 %all-to-all-start = ((bf16[8,1,2,2,64,512]{5,4,2,3,1,0:T(8,128)(2,1)}), bf16[8,1,2,2,64,512]{5,4,2,3,1,0:T(8,128)(2,1)}, u32[]{:S(2)}, u32[]{:S(2)}) async-start(bf16[8,1,2,2,64,512]{5,4,2,3,1,0:T(8,128)(2,1)} %broadcast_in_dim.6), calls=%async_computation | async-start | bytes 4194304 | tf_op jit(solution)/shard_map/all_to_all | solution.py:25
  37.7 13.3 %collective-permute-start = (bf16[1]{0:T(256)(128)(2,1)}, bf16[1]{0:T(256)(128)(2,1)}, u32[]{:S(2)}, u32[]{:S(2)}) collective-permute-start(bf16[1]{0:T(256)(128)(2,1)} %convert_element_type.41), channel_id=1, source_target_pairs={{0,8},{8,16},{16,24},{24,32},{32,40},{40,48},{48,56},{56,64},{64,7... | collective-permute-start | bytes 14 | tf_op jit(solution)/shard_map/ppermute | solution.py:34
  51.0 1.9 collective-permute-start.3
  53.8 2.2 %collective-permute-start.2 = (bf16[1]{0:T(256)(128)(2,1)}, bf16[1]{0:T(256)(128)(2,1)}, u32[]{:S(2)}, u32[]{:S(2)}) collective-permute-start(bf16[1]{0:T(256)(128)(2,1)} %collective-permute-done), channel_id=1, source_target_pairs={{0,8},{8,16},{16,24},{24,32},{32,40},{40,48},{48,56},{56,64},{64,7... | collective-permute-start | bytes 14 | tf_op jit(solution)/shard_map/ppermute | solution.py:34
  56.0 12.6 %collective-permute-done.2 = bf16[1]{0:T(256)(128)(2,1)} collective-permute-done((bf16[1]{0:T(256)(128)(2,1)}, bf16[1]{0:T(256)(128)(2,1)}, u32[]{:S(2)}, u32[]{:S(2)}) %collective-permute-start.2) | collective-permute-done | bytes 34 | tf_op jit(solution)/shard_map/ppermute | solution.py:34
  69.3 1.5 copy.41
  70.9 2.8 %copy.42 = bf16[2,2,512,512]{2,3,0,1:T(8,128)(2,1)S(1)} copy(bf16[2,2,512,512]{3,2,1,0:T(8,128)(2,1)} %bitcast.142) | data formatting | bytes 4194304 | tf_op jit(solution)/shard_map/squeeze;reshape | solution.py:80
  73.7 1.6 broadcast_in_dim.15
  75.2 7.2 %all-to-all-start.2 = ((bf16[8,1,2,2,64,512]{5,4,2,3,1,0:T(8,128)(2,1)}), bf16[8,1,2,2,64,512]{5,4,2,3,1,0:T(8,128)(2,1)}, u32[]{:S(2)}, u32[]{:S(2)}) async-start(bf16[8,1,2,2,64,512]{5,4,2,3,1,0:T(8,128)(2,1)} %broadcast_in_dim.15), calls=%async_computation.2 | async-start | bytes 4194304 | tf_op jit(solution)/shard_map/all_to_all | solution.py:25
  82.5 1.5 slice_bitcast_fusion.2
  84.0 1.8 copy.36
  87.7 16.7 %all-to-all-done.2 = bf16[8,1,2,2,64,512]{5,4,2,3,1,0:T(8,128)(2,1)} async-done(((bf16[8,1,2,2,64,512]{5,4,2,3,1,0:T(8,128)(2,1)}), bf16[8,1,2,2,64,512]{5,4,2,3,1,0:T(8,128)(2,1)}, u32[]{:S(2)}, u32[]{:S(2)}) %all-to-all-start.2) | async-done | bytes 2097184 | tf_op jit(solution)/shard_map/all_to_all | solution.py:25
  104.4 1.8 copy.48
  108.5 1.1 copy-done.1
  116.9 62.0 %psum.35 = f32[2,16,2]{1,0,2:T(2,128)S(1)} all-reduce(f32[2,16,2]{1,0,2:T(2,128)S(1)} %pad_maximum_fusion), channel_id=1, replica_groups=mesh['tm_0'=32,'tm_1'=2,'tm_2'=2,'op_0'=2,'op_1'=4] {'tm_0'}, use_global_device_ids=true, to_apply=%region_0.0 | all-reduce | flops 64 | bytes 512 | tf_op jit(solution)/shard_map/psum | solution.py:38
  178.9 4.3 %psum.36 = f32[2,16,2]{1,0,2:T(2,128)S(1)} all-reduce(f32[2,16,2]{1,0,2:T(2,128)S(1)} %psum.35), channel_id=1, replica_groups=mesh['tm_0'=32,'tm_1'=2,'tm_2'=2,'op_0'=2,'op_1'=4] {'tm_1'}, use_global_device_ids=true, to_apply=%region_1.0 | all-reduce | flops 64 | bytes 512 | tf_op jit(solution)/shard_map/psum | solution.py:38
  183.2 19.7 %psum.37 = f32[2,16,2]{1,0,2:T(2,128)S(1)} all-reduce(f32[2,16,2]{1,0,2:T(2,128)S(1)} %psum.36), channel_id=1, replica_groups=mesh['tm_0'=32,'tm_1'=2,'tm_2'=2,'op_0'=2,'op_1'=4] {'tm_2'}, use_global_device_ids=true, to_apply=%region_2.0 | all-reduce | flops 64 | bytes 512 | tf_op jit(solution)/shard_map/psum | solution.py:38
  202.9 5.3 %psum.38 = f32[2,16,2]{1,0,2:T(2,128)S(1)} all-reduce(f32[2,16,2]{1,0,2:T(2,128)S(1)} %psum.37), channel_id=1, replica_groups=mesh['tm_0'=32,'tm_1'=2,'tm_2'=2,'op_0'=2,'op_1'=4] {'op_0'}, use_global_device_ids=true, to_apply=%region_3.0 | all-reduce | flops 64 | bytes 512 | tf_op jit(solution)/shard_map/psum | solution.py:38
  208.2 8.4 %psum.39 = f32[2,16,2]{1,0,2:T(2,128)S(1)} all-reduce(f32[2,16,2]{1,0,2:T(2,128)S(1)} %psum.38), channel_id=1, replica_groups=mesh['tm_0'=32,'tm_1'=2,'tm_2'=2,'op_0'=2,'op_1'=4] {'op_1'}, use_global_device_ids=true, to_apply=%region_4.0 | all-reduce | flops 64 | bytes 512 | tf_op jit(solution)/shard_map/psum | solution.py:38
  (62 shorter events, 12.4 us)
Async XLA Ops:
  2.5 7.6 %copy-start.7 = (bf16[1,2,2,64,512]{4,3,2,1,0:T(8,128)(2,1)S(1)}, bf16[1,2,2,64,512]{4,3,2,1,0:T(8,128)(2,1)}, u32[]{:S(2)}) copy-start(bf16[1,2,2,64,512]{4,3,2,1,0:T(8,128)(2,1)} %param.6) | copy-start | bytes 786436
  2.5 26.1 %all-to-all-start.1 = ((bf16[8,1,2,2,64,512]{5,4,3,2,1,0:T(8,128)(2,1)}), bf16[8,1,2,2,64,512]{5,4,3,2,1,0:T(8,128)(2,1)S(1)}, u32[]{:S(2)}, u32[]{:S(2)}) async-start(bf16[8,1,2,2,64,512]{5,4,3,2,1,0:T(8,128)(2,1)} %broadcast_in_dim.14), calls=%async_computation.1 | async-start | bytes 4194304 | tf_op jit(solution)/shard_map/all_to_all | solution.py:25
  10.1 18.5 %collective-permute-start.1 = (bf16[1,2,2,64,512]{4,3,2,1,0:T(8,128)(2,1)S(1)}, bf16[1,2,2,64,512]{4,3,2,1,0:T(8,128)(2,1)S(1)}, u32[]{:S(2)}, u32[]{:S(2)}) collective-permute-start(bf16[1,2,2,64,512]{4,3,2,1,0:T(8,128)(2,1)S(1)} %copy-done.7), channel_id=1, source_target_pairs={{0,8},{8,16},{16,24},{24,32},{32,40},{40,48},{48,56},{56,64},{64,7... | collective-permute-start | bytes 786440 | tf_op jit(solution)/shard_map/ppermute | solution.py:34
  30.2 20.8 %copy-start.6 = (s32[128,4]{0,1:T(4,128)S(1)}, s32[128,4]{0,1:T(4,128)}, u32[]{:S(2)}) copy-start(s32[128,4]{0,1:T(4,128)} %param.8) | copy-start | bytes 6148
  30.2 22.7 %copy-start.8 = (s32[128]{0:T(128)S(1)}, s32[128]{0:T(128)}, u32[]{:S(2)}) copy-start(s32[128]{0:T(128)} %param.9) | copy-start | bytes 1540
  30.2 23.0 %copy-start = (bf16[1,2,2,64,512]{4,3,2,1,0:T(8,128)(2,1)S(1)}, bf16[1,2,2,64,512]{4,3,2,1,0:T(8,128)(2,1)}, u32[]{:S(2)}) copy-start(bf16[1,2,2,64,512]{4,3,2,1,0:T(8,128)(2,1)} %param.5) | copy-start | bytes 786436
  30.2 43.5 %all-to-all-start = ((bf16[8,1,2,2,64,512]{5,4,2,3,1,0:T(8,128)(2,1)}), bf16[8,1,2,2,64,512]{5,4,2,3,1,0:T(8,128)(2,1)}, u32[]{:S(2)}, u32[]{:S(2)}) async-start(bf16[8,1,2,2,64,512]{5,4,2,3,1,0:T(8,128)(2,1)} %broadcast_in_dim.6), calls=%async_computation | async-start | bytes 4194304 | tf_op jit(solution)/shard_map/all_to_all | solution.py:25
  37.7 15.6 %collective-permute-start = (bf16[1]{0:T(256)(128)(2,1)}, bf16[1]{0:T(256)(128)(2,1)}, u32[]{:S(2)}, u32[]{:S(2)}) collective-permute-start(bf16[1]{0:T(256)(128)(2,1)} %convert_element_type.41), channel_id=1, source_target_pairs={{0,8},{8,16},{16,24},{24,32},{32,40},{40,48},{48,56},{56,64},{64,7... | collective-permute-start | bytes 14 | tf_op jit(solution)/shard_map/ppermute | solution.py:34
  51.0 18.3 %collective-permute-start.3 = (bf16[1,2,2,64,512]{4,3,2,1,0:T(8,128)(2,1)S(1)}, bf16[1,2,2,64,512]{4,3,2,1,0:T(8,128)(2,1)S(1)}, u32[]{:S(2)}, u32[]{:S(2)}) collective-permute-start(bf16[1,2,2,64,512]{4,3,2,1,0:T(8,128)(2,1)S(1)} %collective-permute-done.1), channel_id=1, source_target_pairs={{0,8},{8,16},{16,24},{24,32},{32,40},{40,48},{48,56},{56,64},{64,7... | collective-permute-start | bytes 786440 | tf_op jit(solution)/shard_map/ppermute | solution.py:34
  53.2 32.7 %copy-start.4 = (bf16[2,64,512]{2,1,0:T(8,128)(2,1)}, bf16[2,64,512]{2,1,0:T(8,128)(2,1)S(1)}, u32[]{:S(2)}) copy-start(bf16[2,64,512]{2,1,0:T(8,128)(2,1)S(1)} %get-tuple-element.24) | copy-start | bytes 393220
  53.8 14.8 %collective-permute-start.2 = (bf16[1]{0:T(256)(128)(2,1)}, bf16[1]{0:T(256)(128)(2,1)}, u32[]{:S(2)}, u32[]{:S(2)}) collective-permute-start(bf16[1]{0:T(256)(128)(2,1)} %collective-permute-done), channel_id=1, source_target_pairs={{0,8},{8,16},{16,24},{24,32},{32,40},{40,48},{48,56},{56,64},{64,7... | collective-permute-start | bytes 14 | tf_op jit(solution)/shard_map/ppermute | solution.py:34
  75.2 29.2 %all-to-all-start.2 = ((bf16[8,1,2,2,64,512]{5,4,2,3,1,0:T(8,128)(2,1)}), bf16[8,1,2,2,64,512]{5,4,2,3,1,0:T(8,128)(2,1)}, u32[]{:S(2)}, u32[]{:S(2)}) async-start(bf16[8,1,2,2,64,512]{5,4,2,3,1,0:T(8,128)(2,1)} %broadcast_in_dim.15), calls=%async_computation.2 | async-start | bytes 4194304 | tf_op jit(solution)/shard_map/all_to_all | solution.py:25
  106.5 0.9 copy-start.5
  108.3 1.2 copy-start.1
  108.3 1.5 copy-start.2
  110.7 1.0 copy-start.3
where the time goes:
time: 219 us; the launch traced here: 217 us
  blocking collectives  99.7 us (46%)
  waiting for transfers between devices  44.7 us (20%)
  starting transfers between devices  42 us (19%)
  local copies, waits for them, and re-layouts  19.6 us (9%)
  matrix products  8.58 us (4%)
  between operations  2.27 us (1%)
    psum x5, blocking collectives, by_axis(): return functools.reduce(lax.psum, axes, array)  99.7 us
    ppermute x4, waiting for transfers between devices, shifted(): lax.ppermute(array, axis, [(i, (i + by) % devices) for i in range(devices)])  28 us
    all_to_all x3, starting transfers between devices, sent_to_all(): return lax.all_to_all(copies, axis, split_axis=0, concat_axis=0, tiled=True)  21.6 us
    ppermute x4, starting transfers between devices, shifted(): lax.ppermute(array, axis, [(i, (i + by) % devices) for i in range(devices)])  20.5 us
    all_to_all x3, waiting for transfers between devices, sent_to_all(): return lax.all_to_all(copies, axis, split_axis=0, concat_axis=0, tiled=True)  16.7 us
    broadcast_in_dim x3, local copies, waits for them, and re-layouts, sent_to_all(): copies = jnp.broadcast_to(array, (lax.axis_size(axis), *array.shape))  5.66 us
  transfers between devices with their start and end apart: 7, of which 3 were waited for; matrix products, arithmetic and copies ran while one was open for 5% of the time, Pallas kernels for 0%

commit v1 on v0

v1 whole, which is shorter than its diff:
```python
import functools
import math

import jax
import jax.numpy as jnp
from jax import lax
from jax.experimental import pallas as pl
from jax.experimental.pallas import tpu as pltpu
from jax.sharding import PartitionSpec as P

WIN = 2
NF = 2
NCORR = 16
PLANE = 4
MESH = pl.DeviceIdType.MESH


def kernel(
    ntm,
    nop,
    sink_hbm,
    source_hbm,
    live_hbm,
    factors_hbm,
    target_hbm,
    out_ref,
    rfull,
    sbuf,
    prod,
    psend,
    recv,
    row,
    row_op,
    row_lo,
    row_z,
    live,
    factors,
    target,
    local_sem,
    gather_send,
    gather_recv,
    shift_send,
    shift_recv,
    block_send,
    block_recv,
    red_send,
    red_recv,
    token,
):
    nz = ntm // PLANE
    rows = source_hbm.shape[3]
    width = source_hbm.shape[4]
    tm = lax.axis_index("tm")
    op = lax.axis_index("op")
    zz = tm // PLANE
    lo = tm - zz * PLANE

    def tm_at(offset):
        return lax.rem(tm + (offset + ntm), ntm)

    def op_at(offset):
        return lax.rem(op + (offset + nop), nop)

    recv[...] = jnp.zeros_like(recv)

    barrier = pltpu.get_barrier_semaphore()
    near = [o for d in range(1, PLANE + 1) for o in (d, -d)]
    for offset in near:
        pl.semaphore_signal(barrier, inc=1, device_id=(tm_at(offset), op), device_id_type=MESH)
    for d in range(1, nop):
        pl.semaphore_signal(barrier, inc=1, device_id=(tm, op_at(d)), device_id_type=MESH)

    my_rows = pl.ds(pl.multiple_of(op * rows, rows), rows)
    local = [
        pltpu.make_async_copy(source_hbm.at[0], rfull.at[:, :, my_rows, :], local_sem.at[0]),
        pltpu.make_async_copy(live_hbm, live, local_sem.at[1]),
        pltpu.make_async_copy(factors_hbm, factors, local_sem.at[2]),
        pltpu.make_async_copy(target_hbm, target, local_sem.at[3]),
    ]
    for copy in local:
        copy.start()

    pl.semaphore_wait(barrier, len(near) + nop - 1)

    gathers = []
    for d in range(1, nop):
        gathers.append(
            pltpu.make_async_remote_copy(
                src_ref=source_hbm.at[0],
                dst_ref=rfull.at[:, :, my_rows, :],
                send_sem=gather_send.at[d],
                recv_sem=gather_recv.at[d],
                device_id=(tm, op_at(d)),
                device_id_type=MESH,
            )
        )
    shifts = []
    for w in range(WIN):
        shifts.append(
            pltpu.make_async_remote_copy(
                src_ref=sink_hbm.at[0],
                dst_ref=sbuf.at[w],
                send_sem=shift_send.at[w],
                recv_sem=shift_recv.at[w],
                device_id=(tm_at(-1 - w), op),
                device_id_type=MESH,
            )
        )
    for copy in gathers + shifts:
        copy.start()

    known = 1
    step = 0
    while known < nz // 2:
        for way in (1, -1):
            pl.semaphore_signal(
                token.at[step],
                inc=1,
                device_id=(tm_at(way * PLANE * known), op),
                device_id_type=MESH,
            )
        pl.semaphore_wait(token.at[step], 2)
        known *= 2
        step += 1

    for copy in local:
        copy.wait()

    fac = factors[...]
    codes = fac[0:1] * (2 * NF * NF) + fac[1:2] * (NF * NF) + fac[2:3] * NF + fac[3:4]
    swapped = fac[2:3] * (2 * NF * NF) + fac[3:4] * (NF * NF) + fac[0:1] * NF + fac[1:2]
    chains = codes.shape[1]
    lane_row = lax.broadcasted_iota(jnp.int32, (128, chains), 0)
    lane_ab = lax.rem(lane_row // 8, 4)
    lane_cd = lax.rem(lane_row, 4)
    lane_code = lane_ab * 4 + lane_cd
    hits = (codes == lane_code).astype(jnp.float32) + (swapped == lane_code).astype(jnp.float32)
    target_hits = (
        target[...] == lax.broadcasted_iota(jnp.int32, (NCORR, chains), 0)
    ).astype(jnp.float32)
    selector = lax.dot_general(
        target_hits.astype(jnp.bfloat16),
        hits.astype(jnp.bfloat16),
        (((1,), (1,)), ((), ())),
        preferred_element_type=jnp.float32,
    )
    weight = live[0].astype(jnp.float32)

    for copy in gathers + shifts:
        copy.wait()

    lhs_real = sbuf[:, :, 0].reshape(WIN * NF * rows, width)
    lhs_imag = sbuf[:, :, 1].reshape(WIN * NF * rows, width)
    half = min(256, width)
    for n in range(width // half):
        cols = slice(n * half, (n + 1) * half)
        for b in range(NF):
            right_real = rfull[b, 0, :, cols]
            right_imag = rfull[b, 1, :, cols]

            def mul(x, y):
                return jnp.dot(x, y, preferred_element_type=jnp.float32)

            real = mul(lhs_real, right_real) - mul(lhs_imag, right_imag)
            imag = mul(lhs_real, right_imag) + mul(lhs_imag, right_real)
            prod[:, 0, :, b, :, cols] = real.astype(jnp.bfloat16).reshape(WIN, NF, rows, half)
            prod[:, 1, :, b, :, cols] = imag.astype(jnp.bfloat16).reshape(WIN, NF, rows, half)

    left = lax.broadcasted_iota(jnp.int32, (rows, 128), 1) < rows
    for w in range(WIN):
        for part in range(2):
            for a in range(NF):
                for tile in range(width // 128):
                    lanes = slice(tile * 128, (tile + 1) * 128)
                    first = prod[w, part, a, 0, :, lanes].astype(jnp.float32)
                    second = prod[w, part, a, 1, :, lanes].astype(jnp.float32)
                    even = jnp.where(left, first, pltpu.roll(second, rows, 1))
                    odd = jnp.where(left, pltpu.roll(first, rows, 1), second)
                    psend[2 * tile, w, a * 2 + part] = even.astype(jnp.bfloat16)
                    psend[2 * tile + 1, w, a * 2 + part] = odd.astype(jnp.bfloat16)

    blocks = []
    for d in range(1, nop // 2):
        dest = op_at(-d)
        blocks.append(
            pltpu.make_async_remote_copy(
                src_ref=psend.at[dest],
                dst_ref=recv.at[:, :, my_rows, :],
                send_sem=block_send.at[d],
                recv_sem=block_recv.at[d],
                device_id=(tm, dest),
                device_id_type=MESH,
            )
        )
    facing = op_at(nop // 2)
    facing_win = facing // (nop // 2)
    blocks.append(
        pltpu.make_async_remote_copy(
            src_ref=psend.at[facing, facing_win],
            dst_ref=recv.at[facing_win, :, my_rows, :],
            send_sem=block_send.at[nop // 2],
            recv_sem=block_recv.at[nop // 2],
            device_id=(tm, facing),
            device_id_type=MESH,
        )
    )
    for copy in blocks:
        copy.start()
    recv[:, :, my_rows, :] = psend[op] * jnp.bfloat16(0.5)
    for copy in blocks:
        copy.wait()

    total = jnp.zeros((8, 128), jnp.float32)
    place_row = lax.broadcasted_iota(jnp.int32, (8, 128), 0)
    place_lane = lax.broadcasted_iota(jnp.int32, (8, 128), 1)
    diagonal = lax.broadcasted_iota(jnp.int32, (rows, 256), 0) == lax.rem(
        lax.broadcasted_iota(jnp.int32, (rows, 256), 1), rows
    )
    for w in range(WIN):
        own = prod[w].reshape(2 * NF * NF * rows, width)
        for c in range(NF):
            right = jnp.concatenate([recv[w, 2 * c], recv[w, 2 * c + 1]], axis=-1)
            square = jnp.dot(own, right, preferred_element_type=jnp.float32)
            kept = jnp.where(diagonal, square.reshape(2 * NF * NF, rows, 256), 0.0).sum(axis=1)
            with_real = kept[:, :128]
            with_imag = kept[:, 128:]
            real = with_real[:4] - with_imag[4:]
            imag = with_imag[:4] + with_real[4:]
            both = jnp.concatenate([real, imag], axis=0)
            for d in range(NF):
                inside = (place_lane >= d * 64) & (place_lane < (d + 1) * 64)
                value = jnp.where(inside, both, 0.0).sum(axis=1, keepdims=True)
                slot = place_lane == place_row * 8 + (w * 4 + c * 2 + d)
                total = total + jnp.where(slot, value, 0.0)
    row[...] = total.sum(axis=0, keepdims=True) * weight

    def exchange(buffer, me, peers, sem):
        buffer[me] = row[...]
        copies = []
        for peer, device in peers:
            copies.append(
                pltpu.make_async_remote_copy(
                    src_ref=row,
                    dst_ref=buffer.at[me],
                    send_sem=red_send.at[sem],
                    recv_sem=red_recv.at[sem],
                    device_id=device,
                    device_id_type=MESH,
                )
            )
        for copy in copies:
            copy.start()
        many = buffer.at[pl.ds(0, len(peers))]
        pltpu.make_async_copy(many, many, red_recv.at[sem]).wait()
        pltpu.make_async_copy(many, many, red_send.at[sem]).wait()
        row[...] = buffer[...].sum(axis=0)

    exchange(row_op, op, [(d, (tm, op_at(d))) for d in range(1, nop)], 0)
    exchange(
        row_lo,
        lo,
        [(d, (zz * PLANE + lax.rem(lo + d, PLANE), op)) for d in range(1, PLANE)],
        1,
    )
    exchange(row_z, zz, [(d, (tm_at(d * PLANE), op)) for d in range(1, nz)], 2)

    spread = row[...] * selector * (1.0 / math.sqrt(ntm))
    lane = lax.broadcasted_iota(jnp.int32, (NCORR, 128), 1)
    for part in range(2):
        for w in range(WIN):
            mine = (lane // 32 == part) & (lax.rem(lane // 4, 2) == w)
            out_ref[part, :, w : w + 1] = jnp.where(mine, spread, 0.0).sum(axis=1, keepdims=True)


def per_device(ntm, nop, sink, source, live, factors, target):
    rows, width = sink.shape[3], sink.shape[4]
    chains = target.shape[0]
    any_space = pl.BlockSpec(memory_space=pl.ANY)
    dma = pltpu.SemaphoreType.DMA
    return pl.pallas_call(
        functools.partial(kernel, ntm, nop),
        out_shape=jax.ShapeDtypeStruct((2, NCORR, WIN), jnp.float32),
        in_specs=[any_space] * 5,
        out_specs=pl.BlockSpec(memory_space=pltpu.VMEM),
        scratch_shapes=[
            pltpu.VMEM((NF, 2, width, width), jnp.bfloat16),
            pltpu.VMEM((WIN, NF, 2, rows, width), jnp.bfloat16),
            pltpu.VMEM((WIN, 2, NF, NF, rows, width), jnp.bfloat16),
            pltpu.VMEM((nop, WIN, 2 * NF, rows, 128), jnp.bfloat16),
            pltpu.VMEM((WIN, 2 * NF, width, 128), jnp.bfloat16),
            pltpu.VMEM((1, 128), jnp.float32),
            pltpu.VMEM((nop, 1, 128), jnp.float32),
            pltpu.VMEM((PLANE, 1, 128), jnp.float32),
            pltpu.VMEM((ntm // PLANE, 1, 128), jnp.float32),
            pltpu.SMEM((1,), jnp.int32),
            pltpu.VMEM((4, chains), jnp.int32),
            pltpu.VMEM((1, chains), jnp.int32),
            dma((4,)),
            dma((nop,)),
            dma((nop,)),
            dma((WIN,)),
            dma((WIN,)),
            dma((nop,)),
            dma((nop,)),
            dma((3,)),
            dma((3,)),
            pltpu.SemaphoreType.REGULAR((8,)),
        ],
        compiler_params=pltpu.CompilerParams(
            collective_id=0, has_side_effects=True, vmem_limit_bytes=48 << 20
        ),
        name="correlate",
    )(sink, source, live, factors.T, target.reshape(1, chains))


def solution(mesh):
    ntm, nop = mesh.shape["tm"], mesh.shape["op"]
    return jax.shard_map(
        functools.partial(per_device, ntm, nop),
        mesh=mesh,
        in_specs=(
            P("tm", None, None, "op", None),
            P("tm", None, None, "op", None),
            P("tm"),
            P(),
            P(),
        ),
        out_specs=P(),
        check_vma=False,
    )
```

time: 219 us -> 98 us (0.45)
  blocking collectives: 99.7 us -> 0 us
  Pallas kernels: 0 us -> 93.1 us
  waiting for transfers between devices: 44.7 us -> 0 us
  starting transfers between devices: 42 us -> 0 us
  local copies, waits for them, and re-layouts: 19.6 us -> 3.23 us
  matrix products: 8.58 us -> 0 us
    psum x5 -> x0, blocking collectives: 99.7 us -> none  [by_axis(): return functools.reduce(lax.psum, axes, array)]
    pallas_call x0 -> x1, Pallas kernels: none -> 93.1 us  [per_device(): pl.pallas_call(functools.partial(kernel, ntm, nop), out_shape=jax.ShapeDt...]
    ppermute x4 -> x0, waiting for transfers between devices: 28 us -> none  [shifted(): lax.ppermute(array, axis, [(i, (i + by) % devices) for i in range(devices)])]
    all_to_all x3 -> x0, starting transfers between devices: 21.6 us -> none  [sent_to_all(): return lax.all_to_all(copies, axis, split_axis=0, concat_axis=0, tiled=True)]
    ppermute x4 -> x0, starting transfers between devices: 20.5 us -> none  [shifted(): lax.ppermute(array, axis, [(i, (i + by) % devices) for i in range(devices)])]
    all_to_all x3 -> x0, waiting for transfers between devices: 16.7 us -> none  [sent_to_all(): return lax.all_to_all(copies, axis, split_axis=0, concat_axis=0, tiled=True)]
    dot_general x15 -> x0, matrix products: 8.58 us -> none  [the longest x2 1.87 us: pair_traces(): jnp.einsum('arx,bxy->abry', sink_stack, source_block, preferred_element_t...]
    broadcast_in_dim x3 -> x0, local copies, waits for them, and re-layouts: 5.66 us -> none  [sent_to_all(): copies = jnp.broadcast_to(array, (lax.axis_size(axis), *array.shape))]
  transfers between devices with their start and end apart: 7 -> 0, of which waited for: 3 -> 0; matrix products, arithmetic and copies ran while one was open for 5% -> 0% of each run, Pallas kernels for 0% -> 0%
where the time goes in v1:
time: 98 us; the launch traced here: 97 us
  Pallas kernels  93.1 us (95%)
  local copies, waits for them, and re-layouts  3.23 us (3%)
    pallas_call x1, Pallas kernels, per_device(): pl.pallas_call(functools.partial(kernel, ntm, nop), out_shape=jax.ShapeDt...  93.1 us
    unnamed x8, local copies, waits for them, and re-layouts  2.57 us

profile of v1, /device:TPU:1, one launch (start us, length us, event | category | flops | bytes accessed | tf_op | source)
XLA Modules:
  0.0 97.0 jit_solution(1241629298512343819)
XLA Ops:
  0.7 0.0 copy-start.2
  0.7 0.0 copy-start.3
  0.7 0.7 copy-done.2
  1.3 0.0 copy-done.3
  1.3 0.0 copy-start
  1.3 0.9 copy-done
  2.3 0.0 copy-start.1
  2.3 0.9 copy-done.1
  3.2 93.1 %correlate.1 = f32[2,16,2]{2,1,0:T(8,128)S(1)} custom-call(bf16[1,2,2,64,512]{4,3,2,1,0:T(8,128)(2,1)S(1)} %copy-done, bf16[1,2,2,64,512]{4,3,2,1,0:T(8,128)(2,1)S(1)} %copy-done.1, s32[1]{0:T(128)S(6)} %copy.7.live_hbm, s32[4,128]{1,0:T(4,128)S(1)} %bitcast.2, s32[1,128]{1,0:T(1,128)S(1)} %bitcast.3), custom_call_target="tpu_custom_call" | custom-call | tf_op jit(solution)/shard_map/correlate/pallas_call | solution.py:280
  96.3 0.7 copy.6
Async XLA Ops:
  0.7 0.7 copy-start.2
  0.7 0.7 copy-start.3
  1.3 1.0 copy-start
  2.3 0.9 copy-start.1

commit v2 on v1

v2 whole, which is shorter than its diff:
```python
import functools
import math

import jax
import jax.numpy as jnp
from jax import lax
from jax.experimental import pallas as pl
from jax.experimental.pallas import tpu as pltpu
from jax.sharding import PartitionSpec as P

WIN = 2
NF = 2
NCORR = 16
NX = 4
MESH = pl.DeviceIdType.MESH


def kernel(
    ntm,
    nop,
    sink_hbm,
    source_hbm,
    live_hbm,
    factors_hbm,
    target_hbm,
    out_ref,
    rfull,
    sbuf,
    prod,
    recv,
    row_plane,
    row_z,
    plane,
    line,
    live,
    factors,
    target,
    local_sem,
    source_send,
    source_recv,
    sink_send,
    sink_recv,
    ring_send,
    ring_recv,
    pair_send,
    pair_recv,
    block_send,
    block_recv,
    red_send,
    red_recv,
    token,
):
    nz, ny = ntm // NX, nop // 2
    rows = source_hbm.shape[3]
    tm, op = lax.axis_index("tm"), lax.axis_index("op")
    z, hi = tm // NX, op // ny
    lo, core = lax.rem(tm // 2, 2), lax.rem(tm, 2)
    x, y = hi * 2 + lo, lax.rem(op, ny)
    here = lo * 2 + core

    def at(base, offset, count):
        return lax.rem(base + (offset % count), count)

    def device(z_at, x_at, core_at, y_at):
        return (z_at * NX + lax.rem(x_at, 2) * 2 + core_at, x_at // 2 * ny + y_at)

    def send(src, dst, send_sem, recv_sem, where):
        return pltpu.make_async_remote_copy(
            src_ref=src,
            dst_ref=dst,
            send_sem=send_sem,
            recv_sem=recv_sem,
            device_id=where,
            device_id_type=MESH,
        )

    def arrived(ref, sem):
        pltpu.make_async_copy(ref, ref, sem).wait()

    recv[2] = jnp.zeros(recv.shape[1:], recv.dtype)

    barrier = pltpu.get_barrier_semaphore()
    greeted = 0
    spot = x * 2 + core
    for dz in (0, 1, -1):
        for k in range(1 if dz == 0 else 0, 2 * NX):
            other = at(spot, k, 2 * NX)
            where = device(at(z, dz, nz), other // 2, lax.rem(other, 2), y)
            pl.semaphore_signal(barrier, inc=1, device_id=where, device_id_type=MESH)
            greeted += 1
    for dy in range(1, ny):
        for k in range(2):
            where = device(z, x, at(core, k, 2), at(y, dy, ny))
            pl.semaphore_signal(barrier, inc=1, device_id=where, device_id_type=MESH)
            greeted += 1

    local = [
        pltpu.make_async_copy(live_hbm, live, local_sem.at[0]),
        pltpu.make_async_copy(factors_hbm, factors, local_sem.at[1]),
        pltpu.make_async_copy(target_hbm, target, local_sem.at[2]),
    ]
    for copy in local:
        copy.start()

    pl.semaphore_wait(barrier, greeted)

    def rows_of(index):
        return pl.ds(pl.multiple_of(index * rows, rows), rows)

    outgoing = []

    def launch(src, dst, send_sem, recv_sem, where, mine):
        copy = send(src, dst, send_sem, recv_sem, where)

        @pl.when(mine)
        def _():
            pltpu.make_async_copy(src, dst, recv_sem).start()

        @pl.when(jnp.logical_not(mine))
        def _():
            copy.start()

        outgoing.append((copy, mine))

    for b in range(NF):
        launch(
            source_hbm.at[0, b],
            rfull.at[b, :, rows_of(op), :],
            source_send.at[b],
            source_recv.at[hi],
            device(z, here, b, y),
            (here == x) & (core == b),
        )
    for w in range(WIN):
        back = here - (w + 1)
        wrap = (back < 0).astype(jnp.int32)
        column = back + wrap * NX
        launch(
            sink_hbm.at[0],
            sbuf.at[:, :, rows_of(hi), :],
            sink_send.at[w],
            sink_recv.at[hi],
            device(lax.rem(z + nz - wrap, nz), column, w, y),
            (wrap == 0) & (column == x) & (core == w),
        )

    ring = []
    pairs = []
    left_y, right_y, far_y = at(y, -1, ny), at(y, 1, ny), at(y, 2, ny)

    def chunk(field, half, y_at):
        return rfull.at[field, :, rows_of(half * ny + y_at), :]

    def pass_on(half, y_at, way):
        ref = chunk(core, half, y_at)
        copy = send(
            ref,
            ref,
            ring_send.at[len(ring)],
            ring_recv.at[half * ny + y_at],
            device(z, x, core, at(y, way, ny)),
        )
        copy.start()
        ring.append(copy)

    def share(half, y_at):
        ref = chunk(core, half, y_at)
        index = half * ny + y_at
        copy = send(
            ref,
            ref,
            pair_send.at[index],
            pair_recv.at[index],
            device(z, x, 1 - core, y),
        )
        copy.start()
        pairs.append(copy)

    tokens = []
    known = 1
    while known < nz // 2:
        tokens.append(known)
        known *= 2

    def token_send(step):
        if step < len(tokens):
            for way in (1, -1):
                where = device(at(z, way * tokens[step], nz), x, core, y)
                pl.semaphore_signal(token.at[step], inc=1, device_id=where, device_id_type=MESH)

    def token_wait(step):
        if step < len(tokens):
            pl.semaphore_wait(token.at[step], 2)

    token_send(0)
    first, second = hi, 1 - hi
    arrived(chunk(core, first, y), source_recv.at[first])
    pass_on(first, y, 1)
    pass_on(first, y, -1)
    share(first, y)
    arrived(chunk(core, second, y), source_recv.at[second])
    pass_on(second, y, -1)
    pass_on(second, y, 1)
    share(second, y)
    token_wait(0)
    token_send(1)

    def from_ring(half, y_at, way):
        arrived(chunk(core, half, y_at), ring_recv.at[half * ny + y_at])
        if way:
            pass_on(half, y_at, way)
        share(half, y_at)

    from_ring(first, left_y, 1)
    from_ring(first, right_y, 0)
    from_ring(second, right_y, -1)
    from_ring(second, left_y, 0)
    token_wait(1)
    token_send(2)

    for copy in local:
        copy.wait()
    fac = factors[...]
    codes = fac[1:2] * 8 + fac[0:1] * 4 + fac[3:4] * 2 + fac[2:3]
    swapped = fac[3:4] * 8 + fac[2:3] * 4 + fac[1:2] * 2 + fac[0:1]
    chains = codes.shape[1]
    lane_row = lax.broadcasted_iota(jnp.int32, (128, chains), 0)
    lane_code = lax.rem(lane_row // 8, 4) * 4 + lax.rem(lane_row, 4)
    hits = (codes == lane_code).astype(jnp.float32) + (swapped == lane_code).astype(jnp.float32)
    target_hits = (
        target[...] == lax.broadcasted_iota(jnp.int32, (NCORR, chains), 0)
    ).astype(jnp.float32)
    selector = lax.dot_general(
        target_hits.astype(jnp.bfloat16),
        hits.astype(jnp.bfloat16),
        (((1,), (1,)), ((), ())),
        preferred_element_type=jnp.float32,
    )
    flag = live[0].astype(jnp.float32)

    from_ring(first, far_y, 0)
    from_ring(second, far_y, 0)
    for half in range(2):
        arrived(sbuf.at[:, :, rows_of(half), :], sink_recv.at[half])

    tall = 2 * rows
    lhs_real = sbuf[:, 0].reshape(NF * tall, nop * rows)
    lhs_imag = sbuf[:, 1].reshape(NF * tall, nop * rows)
    left = lax.broadcasted_iota(jnp.int32, (NF * tall, 128), 1) < 64

    def mul(a, b):
        return jnp.dot(a, b, preferred_element_type=jnp.float32)

    def multiply(b):
        for n in range(2):
            low, high = slice(n * 128, n * 128 + 128), slice(n * 128 + 256, n * 128 + 384)
            right_real = jnp.concatenate([rfull[b, 0, :, low], rfull[b, 0, :, high]], axis=-1)
            right_imag = jnp.concatenate([rfull[b, 1, :, low], rfull[b, 1, :, high]], axis=-1)
            real = mul(lhs_real, right_real) - mul(lhs_imag, right_imag)
            imag = mul(lhs_real, right_imag) + mul(lhs_imag, right_real)
            for part, value in enumerate((real, imag)):
                one, two = value[:, :128], value[:, 128:]
                even = jnp.where(left, one, pltpu.roll(two, 64, 1)).astype(jnp.bfloat16)
                odd = jnp.where(left, pltpu.roll(one, 64, 1), two).astype(jnp.bfloat16)
                prod[2 * n, b, part] = even.reshape(NF, tall, 128)
                prod[2 * n + 1, b, part] = odd.reshape(NF, tall, 128)

    step_y = 1 - 2 * core
    giver_y = lax.rem(y + step_y + ny, ny)
    taker_y = lax.rem(y - step_y + ny, ny)
    gives_far = lax.rem(y // 2 + core, 2) == 1
    blocks = []
    far_blocks = []

    def give(b, index):
        near_copy = send(
            prod.at[taker_y, b],
            recv.at[1, b],
            block_send.at[index],
            block_recv.at[index],
            device(z, x, core, taker_y),
        )
        far_copy = send(
            prod.at[far_y, b],
            recv.at[2, b],
            block_send.at[2 + index],
            block_recv.at[2 + index],
            device(z, x, core, far_y),
        )

        @pl.when(gives_far)
        def _():
            far_copy.start()

        near_copy.start()
        blocks.append(near_copy)
        far_blocks.append(far_copy)

    multiply(core)
    for half in range(2):
        for y_at in range(ny):
            arrived(chunk(1 - core, half, y_at), pair_recv.at[half * ny + y_at])
    give(core, 0)
    multiply(1 - core)
    token_wait(2)
    token_send(3)
    give(1 - core, 1)
    recv[0] = prod[y] * jnp.bfloat16(0.5)
    for copy in blocks:
        copy.wait_recv()

    @pl.when(jnp.logical_not(gives_far))
    def _():
        for copy in far_blocks:
            copy.wait_recv()

    order = [(part, b, a) for part in range(2) for b in range(NF) for a in range(NF)]
    own = jnp.concatenate(
        [
            jnp.concatenate([prod[at_y, b, part, a] for part, b, a in order], axis=0)
            for at_y in (y, giver_y, far_y)
        ],
        axis=1,
    )
    place_row = lax.broadcasted_iota(jnp.int32, (8, 128), 0)
    place_lane = lax.broadcasted_iota(jnp.int32, (8, 128), 1)
    diagonal = lax.broadcasted_iota(jnp.int32, (tall, 256), 0) == lax.rem(
        lax.broadcasted_iota(jnp.int32, (tall, 256), 1), 128
    )
    total = jnp.zeros((8, 128), jnp.float32)
    for d in range(NF):
        for c in range(NF):
            right = jnp.concatenate(
                [
                    jnp.concatenate([recv[slot, d, 0, c], recv[slot, d, 1, c]], axis=1)
                    for slot in range(3)
                ],
                axis=0,
            )
            square = mul(own, right).reshape(8, tall, 256)
            kept = jnp.where(diagonal, square, 0.0).sum(axis=1)
            with_real, with_imag = kept[:, :128], kept[:, 128:]
            real = with_real[:4] - with_imag[4:]
            imag = with_imag[:4] + with_real[4:]
            value = jnp.concatenate([real, imag], axis=0).sum(axis=1, keepdims=True)
            slot_at = place_lane == place_row * 8 + (core * 4 + d * 2 + c)
            total = total + jnp.where(slot_at, value, 0.0)
    lane = lax.broadcasted_iota(jnp.int32, (1, 128), 1)
    row_plane[...] = total.sum(axis=0, keepdims=True) + jnp.where(
        lane == 64 + here, flag * (1.0 / nop), 0.0
    )

    def exchange(buffer, me, source, peers, index):
        buffer[me] = source[...]
        for where in peers:
            send(source, buffer.at[me], red_send.at[index], red_recv.at[index], where).start()
        many = buffer.at[pl.ds(0, len(peers))]
        arrived(many, red_recv.at[index])

    def around(d, n):
        return min(d, n - d)

    spots = [(dx, dy, k) for dx in range(NX) for dy in range(ny) for k in range(2)][1:]
    spots.sort(key=lambda s: -(around(s[0], NX) + around(s[1], ny)))
    exchange(
        plane,
        x * nop + core * ny + y,
        row_plane,
        [device(z, at(x, dx, NX), at(core, k, 2), at(y, dy, ny)) for dx, dy, k in spots],
        0,
    )
    sums = [plane[j * nop : (j + 1) * nop].sum(axis=0) for j in range(NX)]
    flags = sums[0] + sums[1] + sums[2] + sums[3]
    weighted = jnp.zeros((1, 128), jnp.float32)
    for j in range(NX):
        alive = jnp.where(lane == 64 + j, flags, 0.0).sum(axis=1, keepdims=True)
        weighted = weighted + alive * sums[j]
    row_z[...] = weighted

    token_wait(3)
    hops = sorted(range(1, nz), key=lambda d: -around(d, nz))
    exchange(line, z, row_z, [device(at(z, d, nz), x, core, y) for d in hops], 1)
    everything = line[...].sum(axis=0)

    pick_row = lax.broadcasted_iota(jnp.int32, (8, 128), 0)
    pick_lane = lax.broadcasted_iota(jnp.int32, (8, 128), 1)
    picked = (pick_lane // 32 == pick_row // 2) & (
        lax.rem(pick_lane // 4, 2) == lax.rem(pick_row, 2)
    )
    spread = jnp.where(picked, everything * (1.0 / math.sqrt(ntm)), 0.0)
    result = lax.dot_general(
        spread,
        selector,
        (((1,), (1,)), ((), ())),
        precision=lax.Precision.HIGHEST,
        preferred_element_type=jnp.float32,
    )
    out_ref[...] = result[:4]

    for copy, mine in outgoing:

        @pl.when(jnp.logical_not(mine))
        def _(copy=copy):
            copy.wait_send()

    for copy in ring + pairs + blocks:
        copy.wait_send()

    @pl.when(gives_far)
    def _():
        for copy in far_blocks:
            copy.wait_send()

    arrived(plane.at[pl.ds(0, len(spots))], red_send.at[0])
    arrived(line.at[pl.ds(0, len(hops))], red_send.at[1])


def per_device(ntm, nop, sink, source, live, factors, target):
    rows, width = sink.shape[3], sink.shape[4]
    chains = target.shape[0]
    hbm = pl.BlockSpec(memory_space=pltpu.HBM)
    dma = pltpu.SemaphoreType.DMA
    out = pl.pallas_call(
        functools.partial(kernel, ntm, nop),
        out_shape=jax.ShapeDtypeStruct((2 * WIN, NCORR), jnp.float32),
        in_specs=[hbm] * 5,
        out_specs=pl.BlockSpec(memory_space=pltpu.VMEM),
        scratch_shapes=[
            pltpu.VMEM((NF, 2, width, width), jnp.bfloat16),
            pltpu.VMEM((NF, 2, 2 * rows, width), jnp.bfloat16),
            pltpu.VMEM((nop // 2, NF, 2, NF, 2 * rows, 128), jnp.bfloat16),
            pltpu.VMEM((3, NF, 2, NF, 2 * rows, 128), jnp.bfloat16),
            pltpu.VMEM((1, 128), jnp.float32),
            pltpu.VMEM((1, 128), jnp.float32),
            pltpu.VMEM((NX * nop, 1, 128), jnp.float32),
            pltpu.VMEM((ntm // NX, 1, 128), jnp.float32),
            pltpu.SMEM((1,), jnp.int32),
            pltpu.VMEM((4, chains), jnp.int32),
            pltpu.VMEM((1, chains), jnp.int32),
            dma((3,)),
            dma((NF,)),
            dma((2,)),
            dma((WIN,)),
            dma((2,)),
            dma((6,)),
            dma((nop,)),
            dma((nop,)),
            dma((nop,)),
            dma((4,)),
            dma((4,)),
            dma((2,)),
            dma((2,)),
            pltpu.SemaphoreType.REGULAR((8,)),
        ],
        compiler_params=pltpu.CompilerParams(
            collective_id=0, has_side_effects=True, vmem_limit_bytes=67043328
        ),
        name="correlate",
    )(sink, source, live, factors.T, target.reshape(1, chains))
    return jnp.moveaxis(out.reshape(2, WIN, NCORR), 1, 2)


def solution(mesh):
    ntm, nop = mesh.shape["tm"], mesh.shape["op"]
    return jax.shard_map(
        functools.partial(per_device, ntm, nop),
        mesh=mesh,
        in_specs=(
            P("tm", None, None, "op", None),
            P("tm", None, None, "op", None),
            P("tm"),
            P(),
            P(),
        ),
        out_specs=P(),
        check_vma=False,
    )
```

time: 98 us -> 73.3 us (0.75)
  Pallas kernels: 93.1 us -> 71.2 us
  local copies, waits for them, and re-layouts: 3.23 us -> 1.26 us
    pallas_call x1, Pallas kernels: 93.1 us -> 71.2 us  [per_device(): pl.pallas_call(functools.partial(kernel, ntm, nop), out_shape=jax.ShapeDt...]
    unnamed x8 -> x1, local copies, waits for them, and re-layouts: 2.57 us -> 1.26 us
where the time goes in v2:
time: 73.3 us; the launch traced here: 73.2 us
  Pallas kernels  71.2 us (97%)
  local copies, waits for them, and re-layouts  1.26 us (2%)
    pallas_call x1, Pallas kernels, per_device(): pl.pallas_call(functools.partial(kernel, ntm, nop), out_shape=jax.ShapeDt...  71.2 us

profile of v2, /device:TPU:1, one launch (start us, length us, event | category | flops | bytes accessed | tf_op | source)
XLA Modules:
  0.0 73.2 jit_solution(18019970094278459667)
XLA Ops:
  0.7 71.2 %correlate.1 = f32[4,16]{1,0:T(4,128)} custom-call(bf16[1,2,2,64,512]{4,3,2,1,0:T(8,128)(2,1)} %sink_hbm.1, bf16[1,2,2,64,512]{4,3,2,1,0:T(8,128)(2,1)} %source_hbm.1, s32[1]{0:T(128)S(6)} %copy.7.live_hbm, s32[4,128]{1,0:T(4,128)} %bitcast.6, s32[1,128]{1,0:T(1,128)} %bitcast.7), custom_call_target="tpu_custom_call" | custom-call | tf_op jit(solution)/shard_map/correlate/pallas_call | solution.py:423
  71.9 1.3 %copy.8 = f32[2,16,2]{1,2,0:T(2,128)} copy(f32[2,16,2]{1,2,0:T(2,128)} %bitcast.5) | data formatting | bytes 512

commit v3 on v2

--- a/solution.py
+++ b/solution.py
@@ -20,7 +20,7 @@
     nop,
     sink_hbm,
     source_hbm,
-    live_hbm,
+    live,
     factors_hbm,
     target_hbm,
     out_ref,
@@ -32,7 +32,6 @@
     row_z,
     plane,
     line,
-    live,
     factors,
     target,
     local_sem,
@@ -77,95 +76,112 @@
     def arrived(ref, sem):
         pltpu.make_async_copy(ref, ref, sem).wait()
 
-    recv[2] = jnp.zeros(recv.shape[1:], recv.dtype)
-
     barrier = pltpu.get_barrier_semaphore()
-    greeted = 0
-    spot = x * 2 + core
-    for dz in (0, 1, -1):
-        for k in range(1 if dz == 0 else 0, 2 * NX):
-            other = at(spot, k, 2 * NX)
-            where = device(at(z, dz, nz), other // 2, lax.rem(other, 2), y)
-            pl.semaphore_signal(barrier, inc=1, device_id=where, device_id_type=MESH)
-            greeted += 1
-    for dy in range(1, ny):
-        for k in range(2):
-            where = device(z, x, at(core, k, 2), at(y, dy, ny))
-            pl.semaphore_signal(barrier, inc=1, device_id=where, device_id_type=MESH)
-            greeted += 1
-
-    local = [
-        pltpu.make_async_copy(live_hbm, live, local_sem.at[0]),
-        pltpu.make_async_copy(factors_hbm, factors, local_sem.at[1]),
-        pltpu.make_async_copy(target_hbm, target, local_sem.at[2]),
-    ]
-    for copy in local:
-        copy.start()
-
-    pl.semaphore_wait(barrier, greeted)
-
-    def rows_of(index):
-        return pl.ds(pl.multiple_of(index * rows, rows), rows)
-
-    outgoing = []
-
-    def launch(src, dst, send_sem, recv_sem, where, mine):
-        copy = send(src, dst, send_sem, recv_sem, where)
-
-        @pl.when(mine)
-        def _():
-            pltpu.make_async_copy(src, dst, recv_sem).start()
-
-        @pl.when(jnp.logical_not(mine))
-        def _():
-            copy.start()
-
-        outgoing.append((copy, mine))
-
-    for b in range(NF):
-        launch(
-            source_hbm.at[0, b],
-            rfull.at[b, :, rows_of(op), :],
-            source_send.at[b],
-            source_recv.at[hi],
-            device(z, here, b, y),
-            (here == x) & (core == b),
-        )
+
+    def greet(where):
+        pl.semaphore_signal(barrier, inc=1, device_id=where, device_id_type=MESH)
+
+    shifts = []
+    greeted = 2 * NX - 1 + 2 * (ny - 1) + 2
     for w in range(WIN):
         back = here - (w + 1)
         wrap = (back < 0).astype(jnp.int32)
         column = back + wrap * NX
+        where = device(lax.rem(z + nz - wrap, nz), column, w, y)
+        shifts.append((where, (wrap == 0) & (column == x) & (core == w)))
+        greeted = greeted + wrap
+
+        @pl.when(wrap == 1)
+        def _(where=where):
+            greet(where)
+
+    sink_time = x + core + 1
+    greeted = greeted + jnp.where(sink_time >= NX, 2, 0)
+
+    @pl.when(sink_time >= NX)
+    def _():
+        for half in range(2):
+            greet((at(z, 1, nz) * NX + sink_time - NX, half * ny + y))
+
+    spot = x * 2 + core
+    for k in range(1, 2 * NX):
+        other = at(spot, k, 2 * NX)
+        greet(device(z, other // 2, lax.rem(other, 2), y))
+    for dy in range(1, ny):
+        for k in range(2):
+            greet(device(z, x, at(core, k, 2), at(y, dy, ny)))
+    for dz in (1, -1):
+        greet(device(at(z, dz, nz), x, core, y))
+
+    local = [
+        pltpu.make_async_copy(factors_hbm, factors, local_sem.at[0]),
+        pltpu.make_async_copy(target_hbm, target, local_sem.at[1]),
+    ]
+    for copy in local:
+        copy.start()
+
+    pl.semaphore_wait(barrier, greeted)
+
+    def rows_of(index):
+        return pl.ds(pl.multiple_of(index * rows, rows), rows)
+
+    outgoing = []
+
+    def launch(src, dst, send_sem, recv_sem, where, mine):
+        copy = send(src, dst, send_sem, recv_sem, where)
+
+        @pl.when(mine)
+        def _():
+            pltpu.make_async_copy(src, dst, recv_sem).start()
+
+        @pl.when(jnp.logical_not(mine))
+        def _():
+            copy.start()
+
+        outgoing.append((copy, mine))
+
+    for b in range(NF):
+        for part in range(2):
+            launch(
+                source_hbm.at[0, b, part],
+                rfull.at[b, part, rows_of(op), :],
+                source_send.at[b * 2 + part],
+                source_recv.at[b * 2 + hi],
+                device(z, here, part, y),
+                (here == x) & (core == part),
+            )
+    for w, (where, mine) in enumerate(shifts):
         launch(
             sink_hbm.at[0],
             sbuf.at[:, :, rows_of(hi), :],
             sink_send.at[w],
             sink_recv.at[hi],
-            device(lax.rem(z + nz - wrap, nz), column, w, y),
-            (wrap == 0) & (column == x) & (core == w),
+            where,
+            mine,
         )
 
     ring = []
     pairs = []
     left_y, right_y, far_y = at(y, -1, ny), at(y, 1, ny), at(y, 2, ny)
 
-    def chunk(field, half, y_at):
-        return rfull.at[field, :, rows_of(half * ny + y_at), :]
-
-    def pass_on(half, y_at, way):
-        ref = chunk(core, half, y_at)
+    def chunk(b, part, half, y_at):
+        return rfull.at[b, part, rows_of(half * ny + y_at), :]
+
+    def pass_on(b, half, y_at, way):
+        ref = chunk(b, core, half, y_at)
         copy = send(
             ref,
             ref,
             ring_send.at[len(ring)],
-            ring_recv.at[half * ny + y_at],
+            ring_recv.at[b * nop + half * ny + y_at],
             device(z, x, core, at(y, way, ny)),
         )
         copy.start()
         ring.append(copy)
 
-    def share(half, y_at):
-        ref = chunk(core, half, y_at)
-        index = half * ny + y_at
+    def share(b, half, y_at):
+        ref = chunk(b, core, half, y_at)
+        index = b * nop + half * ny + y_at
         copy = send(
             ref,
             ref,
@@ -176,6 +192,10 @@
         copy.start()
         pairs.append(copy)
 
+    step_y = 1 - 2 * core
+    giver_y = lax.rem(y + step_y + ny, ny)
+    taker_y = lax.rem(y - step_y + ny, ny)
+    gives_far = lax.rem(y // 2 + core, 2) == 1
     tokens = []
     known = 1
     while known < nz // 2:
@@ -194,29 +214,35 @@
 
     token_send(0)
     first, second = hi, 1 - hi
-    arrived(chunk(core, first, y), source_recv.at[first])
-    pass_on(first, y, 1)
-    pass_on(first, y, -1)
-    share(first, y)
-    arrived(chunk(core, second, y), source_recv.at[second])
-    pass_on(second, y, -1)
-    pass_on(second, y, 1)
-    share(second, y)
+
+    def from_source(b, half, way):
+        arrived(chunk(b, core, half, y), source_recv.at[b * 2 + half])
+        pass_on(b, half, y, way)
+        pass_on(b, half, y, -way)
+        share(b, half, y)
+
+    def from_ring(b, half, y_at, way):
+        arrived(chunk(b, core, half, y_at), ring_recv.at[b * nop + half * ny + y_at])
+        if way:
+            pass_on(b, half, y_at, way)
+        share(b, half, y_at)
+
+    from_source(0, first, 1)
+    from_source(0, second, -1)
+    from_source(1, first, 1)
+    from_ring(0, first, left_y, 1)
+    from_ring(0, second, right_y, -1)
+    from_source(1, second, -1)
     token_wait(0)
     token_send(1)
-
-    def from_ring(half, y_at, way):
-        arrived(chunk(core, half, y_at), ring_recv.at[half * ny + y_at])
-        if way:
-            pass_on(half, y_at, way)
-        share(half, y_at)
-
-    from_ring(first, left_y, 1)
-    from_ring(first, right_y, 0)
-    from_ring(second, right_y, -1)
-    from_ring(second, left_y, 0)
-    token_wait(1)
-    token_send(2)
+    from_ring(0, first, right_y, 0)
+    from_ring(0, second, left_y, 0)
+    from_ring(1, first, left_y, 1)
+    from_ring(1, second, right_y, -1)
+
+    @pl.when(gives_far)
+    def _():
+        recv[2] = jnp.zeros(recv.shape[1:], recv.dtype)
 
     for copy in local:
         copy.wait()
@@ -238,8 +264,10 @@
     )
     flag = live[0].astype(jnp.float32)
 
-    from_ring(first, far_y, 0)
-    from_ring(second, far_y, 0)
+    token_wait(1)
+    token_send(2)
+    from_ring(0, first, far_y, 0)
+    from_ring(0, second, far_y, 0)
     for half in range(2):
         arrived(sbuf.at[:, :, rows_of(half), :], sink_recv.at[half])
 
@@ -265,26 +293,22 @@
                 prod[2 * n, b, part] = even.reshape(NF, tall, 128)
                 prod[2 * n + 1, b, part] = odd.reshape(NF, tall, 128)
 
-    step_y = 1 - 2 * core
-    giver_y = lax.rem(y + step_y + ny, ny)
-    taker_y = lax.rem(y - step_y + ny, ny)
-    gives_far = lax.rem(y // 2 + core, 2) == 1
     blocks = []
     far_blocks = []
 
-    def give(b, index):
+    def give(b):
         near_copy = send(
             prod.at[taker_y, b],
             recv.at[1, b],
-            block_send.at[index],
-            block_recv.at[index],
+            block_send.at[b],
+            block_recv.at[b],
             device(z, x, core, taker_y),
         )
         far_copy = send(
             prod.at[far_y, b],
             recv.at[2, b],
-            block_send.at[2 + index],
-            block_recv.at[2 + index],
+            block_send.at[2 + b],
+            block_recv.at[2 + b],
             device(z, x, core, far_y),
         )
 
@@ -296,23 +320,25 @@
         blocks.append(near_copy)
         far_blocks.append(far_copy)
 
-    multiply(core)
-    for half in range(2):
-        for y_at in range(ny):
-            arrived(chunk(1 - core, half, y_at), pair_recv.at[half * ny + y_at])
-    give(core, 0)
-    multiply(1 - core)
+    def shared(b):
+        for half in range(2):
+            for y_at in range(ny):
+                index = b * nop + half * ny + y_at
+                arrived(chunk(b, 1 - core, half, y_at), pair_recv.at[index])
+
+    shared(0)
+    multiply(0)
+    from_ring(1, first, right_y, 0)
+    from_ring(1, second, left_y, 0)
+    give(0)
+    from_ring(1, first, far_y, 0)
+    from_ring(1, second, far_y, 0)
+    shared(1)
+    multiply(1)
+    recv[0] = prod[y] * jnp.bfloat16(0.5)
+    give(1)
     token_wait(2)
     token_send(3)
-    give(1 - core, 1)
-    recv[0] = prod[y] * jnp.bfloat16(0.5)
-    for copy in blocks:
-        copy.wait_recv()
-
-    @pl.when(jnp.logical_not(gives_far))
-    def _():
-        for copy in far_blocks:
-            copy.wait_recv()
 
     order = [(part, b, a) for part in range(2) for b in range(NF) for a in range(NF)]
     own = jnp.concatenate(
@@ -329,6 +355,12 @@
     )
     total = jnp.zeros((8, 128), jnp.float32)
     for d in range(NF):
+        blocks[d].wait_recv()
+
+        @pl.when(jnp.logical_not(gives_far))
+        def _(d=d):
+            far_blocks[d].wait_recv()
+
         for c in range(NF):
             right = jnp.concatenate(
                 [
@@ -354,8 +386,9 @@
         buffer[me] = source[...]
         for where in peers:
             send(source, buffer.at[me], red_send.at[index], red_recv.at[index], where).start()
-        many = buffer.at[pl.ds(0, len(peers))]
-        arrived(many, red_recv.at[index])
+
+    def exchanged(buffer, peers, index):
+        arrived(buffer.at[pl.ds(0, len(peers))], red_recv.at[index])
 
     def around(d, n):
         return min(d, n - d)
@@ -369,6 +402,7 @@
         [device(z, at(x, dx, NX), at(core, k, 2), at(y, dy, ny)) for dx, dy, k in spots],
         0,
     )
+    exchanged(plane, spots, 0)
     sums = [plane[j * nop : (j + 1) * nop].sum(axis=0) for j in range(NX)]
     flags = sums[0] + sums[1] + sums[2] + sums[3]
     weighted = jnp.zeros((1, 128), jnp.float32)
@@ -380,6 +414,22 @@
     token_wait(3)
     hops = sorted(range(1, nz), key=lambda d: -around(d, nz))
     exchange(line, z, row_z, [device(at(z, d, nz), x, core, y) for d in hops], 1)
+
+    for copy, mine in outgoing:
+
+        @pl.when(jnp.logical_not(mine))
+        def _(copy=copy):
+            copy.wait_send()
+
+    for copy in ring + pairs + blocks:
+        copy.wait_send()
+
+    @pl.when(gives_far)
+    def _():
+        for copy in far_blocks:
+            copy.wait_send()
+
+    exchanged(line, hops, 1)
     everything = line[...].sum(axis=0)
 
     pick_row = lax.broadcasted_iota(jnp.int32, (8, 128), 0)
@@ -397,20 +447,6 @@
     )
     out_ref[...] = result[:4]
 
-    for copy, mine in outgoing:
-
-        @pl.when(jnp.logical_not(mine))
-        def _(copy=copy):
-            copy.wait_send()
-
-    for copy in ring + pairs + blocks:
-        copy.wait_send()
-
-    @pl.when(gives_far)
-    def _():
-        for copy in far_blocks:
-            copy.wait_send()
-
     arrived(plane.at[pl.ds(0, len(spots))], red_send.at[0])
     arrived(line.at[pl.ds(0, len(hops))], red_send.at[1])
 
@@ -420,10 +456,11 @@
     chains = target.shape[0]
     hbm = pl.BlockSpec(memory_space=pltpu.HBM)
     dma = pltpu.SemaphoreType.DMA
+    pin = functools.partial(pltpu.with_memory_space_constraint, memory_space=pltpu.HBM)
     out = pl.pallas_call(
         functools.partial(kernel, ntm, nop),
         out_shape=jax.ShapeDtypeStruct((2 * WIN, NCORR), jnp.float32),
-        in_specs=[hbm] * 5,
+        in_specs=[hbm, hbm, pl.BlockSpec(memory_space=pltpu.SMEM), hbm, hbm],
         out_specs=pl.BlockSpec(memory_space=pltpu.VMEM),
         scratch_shapes=[
             pltpu.VMEM((NF, 2, width, width), jnp.bfloat16),
@@ -434,18 +471,17 @@
             pltpu.VMEM((1, 128), jnp.float32),
             pltpu.VMEM((NX * nop, 1, 128), jnp.float32),
             pltpu.VMEM((ntm // NX, 1, 128), jnp.float32),
-            pltpu.SMEM((1,), jnp.int32),
             pltpu.VMEM((4, chains), jnp.int32),
             pltpu.VMEM((1, chains), jnp.int32),
-            dma((3,)),
-            dma((NF,)),
             dma((2,)),
+            dma((2 * NF,)),
+            dma((2 * NF,)),
             dma((WIN,)),
             dma((2,)),
-            dma((6,)),
-            dma((nop,)),
-            dma((nop,)),
-            dma((nop,)),
+            dma((6 * NF,)),
+            dma((nop * NF,)),
+            dma((nop * NF,)),
+            dma((nop * NF,)),
             dma((4,)),
             dma((4,)),
             dma((2,)),
@@ -453,10 +489,10 @@
             pltpu.SemaphoreType.REGULAR((8,)),
         ],
         compiler_params=pltpu.CompilerParams(
-            collective_id=0, has_side_effects=True, vmem_limit_bytes=67043328
+            collective_id=0, has_side_effects=True, vmem_limit_bytes=48 << 20
         ),
         name="correlate",
-    )(sink, source, live, factors.T, target.reshape(1, chains))
+    )(pin(sink), pin(source), live, pin(factors.T), pin(target.reshape(1, chains)))
     return jnp.moveaxis(out.reshape(2, WIN, NCORR), 1, 2)
 
 

time: 73.3 us -> 70.6 us (0.963)
  Pallas kernels: 71.2 us -> 69.2 us
    pallas_call x1, Pallas kernels: 71.2 us -> 69.2 us  [per_device(): pl.pallas_call(functools.partial(kernel, ntm, nop), out_shape=jax.ShapeDt...]
where the time goes in v3:
time: 70.6 us; the launch traced here: 70.5 us
  Pallas kernels  69.2 us (98%)
    pallas_call x1, Pallas kernels, per_device(): pl.pallas_call(functools.partial(kernel, ntm, nop), out_shape=jax.ShapeDt...  69.2 us

profile of v3, /device:TPU:1, one launch (start us, length us, event | category | flops | bytes accessed | tf_op | source)
XLA Modules:
  0.0 70.5 jit_solution(5333065411124690953)
XLA Ops:
  0.7 69.2 %correlate.1 = f32[4,16]{1,0:T(4,128)S(1)} custom-call(bf16[1,2,2,64,512]{4,3,2,1,0:T(8,128)(2,1)} %sink_hbm.1, bf16[1,2,2,64,512]{4,3,2,1,0:T(8,128)(2,1)} %source_hbm.1, s32[1]{0:T(128)S(6)} %copy.7.live, s32[4,128]{1,0:T(4,128)} %bitcast.6, s32[1,128]{1,0:T(1,128)} %bitcast.7), custom_call_target="tpu_custom_call" | custom-call | tf_op jit(solution)/shard_map/correlate/pallas_call | solution.py:460
  69.9 0.6 copy.8

commit v4 on v3

--- a/solution.py
+++ b/solution.py
@@ -150,16 +150,6 @@
                 device(z, here, part, y),
                 (here == x) & (core == part),
             )
-    for w, (where, mine) in enumerate(shifts):
-        launch(
-            sink_hbm.at[0],
-            sbuf.at[:, :, rows_of(hi), :],
-            sink_send.at[w],
-            sink_recv.at[hi],
-            where,
-            mine,
-        )
-
     ring = []
     pairs = []
     left_y, right_y, far_y = at(y, -1, ny), at(y, 1, ny), at(y, 2, ny)
@@ -229,6 +219,16 @@
 
     from_source(0, first, 1)
     from_source(0, second, -1)
+    for w, (where, mine) in enumerate(shifts):
+        launch(
+            sink_hbm.at[0],
+            sbuf.at[:, :, rows_of(hi), :],
+            sink_send.at[w],
+            sink_recv.at[hi],
+            where,
+            mine,
+        )
+
     from_source(1, first, 1)
     from_ring(0, first, left_y, 1)
     from_ring(0, second, right_y, -1)

time: 70.6 us -> 66.4 us (0.941)
  Pallas kernels: 69.2 us -> 64.9 us
    pallas_call x1, Pallas kernels: 69.2 us -> 64.9 us  [per_device(): pl.pallas_call(functools.partial(kernel, ntm, nop), out_shape=jax.ShapeDt...]
where the time goes in v4:
time: 66.4 us; the launch traced here: 66.2 us
  Pallas kernels  64.9 us (98%)
    pallas_call x1, Pallas kernels, per_device(): pl.pallas_call(functools.partial(kernel, ntm, nop), out_shape=jax.ShapeDt...  64.9 us

profile of v4, /device:TPU:1, one launch (start us, length us, event | category | flops | bytes accessed | tf_op | source)
XLA Modules:
  0.0 66.2 jit_solution(1630713962179236611)
XLA Ops:
  0.7 64.9 %correlate.1 = f32[4,16]{1,0:T(4,128)S(1)} custom-call(bf16[1,2,2,64,512]{4,3,2,1,0:T(8,128)(2,1)} %sink_hbm.1, bf16[1,2,2,64,512]{4,3,2,1,0:T(8,128)(2,1)} %source_hbm.1, s32[1]{0:T(128)S(6)} %copy.7.live, s32[4,128]{1,0:T(4,128)} %bitcast.6, s32[1,128]{1,0:T(1,128)} %bitcast.7), custom_call_target="tpu_custom_call" | custom-call | tf_op jit(solution)/shard_map/correlate/pallas_call | solution.py:460
  65.6 0.6 copy.8

commit v5 on v4

--- a/solution.py
+++ b/solution.py
@@ -57,6 +57,11 @@
     x, y = hi * 2 + lo, lax.rem(op, ny)
     here = lo * 2 + core
 
+    def column_of(j):
+        return lax.rem(2 * j + 1, 5)
+
+    mine_j = lax.rem(3 * x + 2, 5)
+
     def at(base, offset, count):
         return lax.rem(base + (offset % count), count)
 
@@ -86,7 +91,7 @@
     for w in range(WIN):
         back = here - (w + 1)
         wrap = (back < 0).astype(jnp.int32)
-        column = back + wrap * NX
+        column = column_of(back + wrap * NX)
         where = device(lax.rem(z + nz - wrap, nz), column, w, y)
         shifts.append((where, (wrap == 0) & (column == x) & (core == w)))
         greeted = greeted + wrap
@@ -95,7 +100,7 @@
         def _(where=where):
             greet(where)
 
-    sink_time = x + core + 1
+    sink_time = mine_j + core + 1
     greeted = greeted + jnp.where(sink_time >= NX, 2, 0)
 
     @pl.when(sink_time >= NX)
@@ -147,8 +152,8 @@
                 rfull.at[b, part, rows_of(op), :],
                 source_send.at[b * 2 + part],
                 source_recv.at[b * 2 + hi],
-                device(z, here, part, y),
-                (here == x) & (core == part),
+                device(z, column_of(here), part, y),
+                (column_of(here) == x) & (core == part),
             )
     ring = []
     pairs = []
@@ -341,19 +346,26 @@
     token_send(3)
 
     order = [(part, b, a) for part in range(2) for b in range(NF) for a in range(NF)]
-    own = jnp.concatenate(
-        [
-            jnp.concatenate([prod[at_y, b, part, a] for part, b, a in order], axis=0)
-            for at_y in (y, giver_y, far_y)
-        ],
-        axis=1,
-    )
+    own, near, far = [
+        jnp.concatenate([prod[at_y, b, part, a] for part, b, a in order], axis=0)
+        for at_y in (y, giver_y, far_y)
+    ]
+    others = jnp.concatenate([near, far], axis=1)
     place_row = lax.broadcasted_iota(jnp.int32, (8, 128), 0)
     place_lane = lax.broadcasted_iota(jnp.int32, (8, 128), 1)
     diagonal = lax.broadcasted_iota(jnp.int32, (tall, 256), 0) == lax.rem(
         lax.broadcasted_iota(jnp.int32, (tall, 256), 1), 128
     )
     total = jnp.zeros((8, 128), jnp.float32)
+
+    def pair_of(slot, d, c):
+        return jnp.concatenate([recv[slot, d, 0, c], recv[slot, d, 1, c]], axis=1)
+
+    def traced(lhs, rhs):
+        square = mul(lhs, rhs).reshape(8, tall, 256)
+        return jnp.where(diagonal, square, 0.0).sum(axis=1)
+
+    alone = [[traced(own, pair_of(0, d, c)) for c in range(NF)] for d in range(NF)]
     for d in range(NF):
         blocks[d].wait_recv()
 
@@ -362,15 +374,8 @@
             far_blocks[d].wait_recv()
 
         for c in range(NF):
-            right = jnp.concatenate(
-                [
-                    jnp.concatenate([recv[slot, d, 0, c], recv[slot, d, 1, c]], axis=1)
-                    for slot in range(3)
-                ],
-                axis=0,
-            )
-            square = mul(own, right).reshape(8, tall, 256)
-            kept = jnp.where(diagonal, square, 0.0).sum(axis=1)
+            right = jnp.concatenate([pair_of(1, d, c), pair_of(2, d, c)], axis=0)
+            kept = alone[d][c] + traced(others, right)
             with_real, with_imag = kept[:, :128], kept[:, 128:]
             real = with_real[:4] - with_imag[4:]
             imag = with_imag[:4] + with_real[4:]
@@ -407,7 +412,7 @@
     flags = sums[0] + sums[1] + sums[2] + sums[3]
     weighted = jnp.zeros((1, 128), jnp.float32)
     for j in range(NX):
-        alive = jnp.where(lane == 64 + j, flags, 0.0).sum(axis=1, keepdims=True)
+        alive = jnp.where(lane == 64 + (3 * j + 2) % 5, flags, 0.0).sum(axis=1, keepdims=True)
         weighted = weighted + alive * sums[j]
     row_z[...] = weighted
 

time: 66.4 us -> 65.5 us (0.986)
  Pallas kernels: 64.9 us -> 64.1 us
    pallas_call x1, Pallas kernels: 64.9 us -> 64.1 us  [per_device(): pl.pallas_call(functools.partial(kernel, ntm, nop), out_shape=jax.ShapeDt...]
where the time goes in v5:
time: 65.5 us; the launch traced here: 65.3 us
  Pallas kernels  64.1 us (98%)
  between operations  0.66 us (1%)
    pallas_call x1, Pallas kernels, per_device(): pl.pallas_call(functools.partial(kernel, ntm, nop), out_shape=jax.ShapeDt...  64.1 us

profile of v5, /device:TPU:1, one launch (start us, length us, event | category | flops | bytes accessed | tf_op | source)
XLA Modules:
  0.0 65.3 jit_solution(12327510763228251090)
XLA Ops:
  0.7 64.1 %correlate.1 = f32[4,16]{1,0:T(4,128)S(1)} custom-call(bf16[1,2,2,64,512]{4,3,2,1,0:T(8,128)(2,1)} %sink_hbm.1, bf16[1,2,2,64,512]{4,3,2,1,0:T(8,128)(2,1)} %source_hbm.1, s32[1]{0:T(128)S(6)} %copy.7.live, s32[4,128]{1,0:T(4,128)} %bitcast.6, s32[1,128]{1,0:T(1,128)} %bitcast.7), custom_call_target="tpu_custom_call" | custom-call | tf_op jit(solution)/shard_map/correlate/pallas_call | solution.py:465
  64.8 0.6 copy.8

commit v6 on v5

--- a/solution.py
+++ b/solution.py
@@ -235,9 +235,9 @@
         )
 
     from_source(1, first, 1)
+    from_source(1, second, -1)
     from_ring(0, first, left_y, 1)
     from_ring(0, second, right_y, -1)
-    from_source(1, second, -1)
     token_wait(0)
     token_send(1)
     from_ring(0, first, right_y, 0)

time: 65.5 us -> 65.4 us (level)
  no operation moved by 1% of the time
where the time goes in v6:
time: 65.4 us; the launch traced here: 65.3 us
  Pallas kernels  64 us (98%)
  between operations  0.66 us (1%)
    pallas_call x1, Pallas kernels, per_device(): pl.pallas_call(functools.partial(kernel, ntm, nop), out_shape=jax.ShapeDt...  64 us

profile of v6, /device:TPU:1, one launch (start us, length us, event | category | flops | bytes accessed | tf_op | source)
XLA Modules:
  0.0 65.3 jit_solution(13325192595654304375)
XLA Ops:
  0.7 64.0 %correlate.1 = f32[4,16]{1,0:T(4,128)S(1)} custom-call(bf16[1,2,2,64,512]{4,3,2,1,0:T(8,128)(2,1)} %sink_hbm.1, bf16[1,2,2,64,512]{4,3,2,1,0:T(8,128)(2,1)} %source_hbm.1, s32[1]{0:T(128)S(6)} %copy.7.live, s32[4,128]{1,0:T(4,128)} %bitcast.6, s32[1,128]{1,0:T(1,128)} %bitcast.7), custom_call_target="tpu_custom_call" | custom-call | tf_op jit(solution)/shard_map/correlate/pallas_call | solution.py:465
  64.7 0.6 copy.8
